TPU v7x, 32 devices: a whole 2x2x4 slice. The times are simulated.
32 devices in a mesh: aa: 4 (over z), ba: 8 (over y, x, core).
Axes of the slice: x: 2, y: 2, z: 4, core: 2. Of those that a mesh axis runs over, the one named last changes fastest.
Arguments:
- feats: bfloat16 [4, 32, 128, 256], P('aa', 'ba'), may hold values from -6 to 6
- conv_one: bfloat16 [3, 3, 3, 256, 256], replicated, may hold values from -0.078125 to 0.078125
- bias_one: float32 [256], replicated, may hold values from -3 to 3
- conv_two: bfloat16 [3, 3, 3, 256, 256], replicated, may hold values from -0.078125 to 0.078125
- bias_two: float32 [256], replicated, may hold values from -3 to 3
- patch_weight: bfloat16 [2, 2, 256, 128], replicated, may hold values from -0.1875 to 0.1875
- patch_bias: float32 [128], replicated, may hold values from -3 to 3
- embed_weight: bfloat16 [128, 2048], replicated, may hold values from -0.5 to 0.5
- embed_bias: float32 [2048], replicated, may hold values from -6 to 6
- norm_gain: float32 [2048], replicated, may hold values from 0.1 to 1.9
- w_query: bfloat16 [2048, 2048], P(None, 'ba'), may hold values from -2 to 2
- w_key: bfloat16 [2048, 2048], P(None, 'ba'), may hold values from -2 to 2
- w_value: bfloat16 [2048, 2048], P(None, 'ba'), may hold values from -0.125 to 0.125
- w_velocity: bfloat16 [2048, 128], P('ba'), may hold values from -0.5 to 0.5
Outputs:
- velocity: float32 [4096, 128], P(('aa', 'ba'))
All inputs are finite; a program needn't handle non-finite values.
Results may differ from a plain program's by a relative error of at most 0.035.
Values may be sent and summed in bfloat16 or wider, within the bound.
A program may use at most 128 MiB of HBM per device.

v0:
```python
import math
import jax
import jax.numpy as jnp
from jax import lax
from jax.sharding import PartitionSpec as P

HEAD_DIM = 64


def with_halo(cells, sides, width):
    for axis, dim in sides:
        count = lax.axis_size(axis)
        ends = count - 1
        head = lax.slice_in_dim(cells, 0, width, axis=dim)
        tail = lax.slice_in_dim(cells, cells.shape[dim] - width, cells.shape[dim], axis=dim)
        cells = jnp.concatenate(
            [
                lax.ppermute(tail, axis, [(i, (i + 1) % count) for i in range(ends)]),
                cells,
                lax.ppermute(head, axis, [((i + 1) % count, i) for i in range(ends)]),
            ],
            axis=dim,
        )
    return cells


def convolve(field, kernel, bias):
    frames, rows, width, chans = field.shape
    padded = with_halo(field, (("aa", 0), ("ba", 1)), 1)
    padded = jnp.pad(padded, ((0, 0), (0, 0), (1, 1), (0, 0)))
    total = jnp.zeros((frames * rows * width, kernel.shape[-1]), jnp.float32)
    for shift_t in range(3):
        for shift_r in range(3):
            window = padded[shift_t : shift_t + frames, shift_r : shift_r + rows]
            stacked = jnp.concatenate(
                [window[:, :, shift_w : shift_w + width] for shift_w in range(3)], axis=-1
            )
            total = total + jnp.dot(
                stacked.reshape(-1, 3 * chans),
                kernel[shift_t, shift_r].reshape(3 * chans, -1),
                preferred_element_type=jnp.float32,
            )
    return (total + bias).reshape(frames, rows, width, -1)


def patchify(field, weight, bias):
    frames, rows, width, chans = field.shape
    blocks = (
        field.reshape(frames, rows // 2, 2, width // 2, 2, chans)
        .transpose(0, 1, 3, 2, 4, 5)
        .reshape(-1, 4 * chans)
    )
    return (
        jnp.dot(blocks, weight.reshape(4 * chans, -1), preferred_element_type=jnp.float32) + bias
    ).astype(jnp.bfloat16)


def normalize(latent_rows, embed_weight, embed_bias, norm_gain):
    hidden = jnp.dot(latent_rows, embed_weight, preferred_element_type=jnp.float32) + embed_bias
    center = hidden - hidden.mean(-1, keepdims=True)
    spread = (center * center).mean(-1, keepdims=True)
    return (center * lax.rsqrt(spread + 1e-05) * norm_gain).astype(jnp.bfloat16)


def attend(queries, keys, values):
    rows, width = queries.shape
    heads = width // HEAD_DIM
    scale = HEAD_DIM ** (-0.5)
    query_heads = queries.reshape(rows, heads, HEAD_DIM)
    start_state = (
        jnp.full((heads, rows), -jnp.inf, jnp.float32),
        jnp.zeros((heads, rows), jnp.float32),
        jnp.zeros((rows, heads, HEAD_DIM), jnp.float32),
    )
    key_rows = lax.all_gather(keys, "aa", axis=0, tiled=True)
    value_rows = lax.all_gather(values, "aa", axis=0, tiled=True)
    count = key_rows.shape[0]
    block = math.gcd(count, 1024)

    def one_step(index, state):
        best, denom, accum = state
        key_block = lax.dynamic_slice_in_dim(key_rows, index * block, block, 0).reshape(
            block, heads, HEAD_DIM
        )
        value_block = lax.dynamic_slice_in_dim(value_rows, index * block, block, 0).reshape(
            block, heads, HEAD_DIM
        )
        scores = (
            jnp.einsum("qhd,khd->hqk", query_heads, key_block, preferred_element_type=jnp.float32)
            * scale
        )
        peak = jnp.maximum(best, scores.max(-1))
        probs = jnp.exp(scores - peak[..., None])
        fade = jnp.exp(best - peak)
        denom = denom * fade + probs.sum(-1)
        accum = accum * fade.T[..., None] + jnp.einsum(
            "hqk,khd->qhd",
            probs.astype(jnp.bfloat16),
            value_block,
            preferred_element_type=jnp.float32,
        )
        return (peak, denom, accum)

    best, denom, accum = lax.fori_loop(0, count // block, one_step, start_state)
    return (accum / denom.T[..., None]).reshape(rows, width).astype(jnp.bfloat16)


def on_device(
    feats,
    conv_one,
    bias_one,
    conv_two,
    bias_two,
    patch_weight,
    patch_bias,
    embed_weight,
    embed_bias,
    norm_gain,
    w_query,
    w_key,
    w_value,
    w_velocity,
):
    first = jax.nn.gelu(convolve(feats, conv_one, bias_one), approximate=False).astype(jnp.bfloat16)
    second = (
        first.astype(jnp.float32)
        + jax.nn.gelu(convolve(first, conv_two, bias_two), approximate=False)
    ).astype(jnp.bfloat16)
    latents = patchify(second, patch_weight, patch_bias)
    width = w_query.shape[1]
    w_joined = jnp.concatenate([w_query, w_key, w_value], axis=1)
    joined = jnp.dot(
        normalize(
            lax.all_gather(latents, "ba", axis=0, tiled=True), embed_weight, embed_bias, norm_gain
        ),
        w_joined,
        preferred_element_type=jnp.float32,
    ).astype(jnp.bfloat16)
    attended = attend(joined[:, :width], joined[:, width : 2 * width], joined[:, 2 * width :])
    return lax.psum_scatter(
        jnp.dot(attended, w_velocity, preferred_element_type=jnp.float32).astype(jnp.bfloat16),
        "ba",
        scatter_dimension=0,
        tiled=True,
    ).astype(jnp.float32)


def solution(mesh):
    return jax.shard_map(
        on_device,
        mesh=mesh,
        in_specs=(
            P("aa", "ba", None, None),
            P(),
            P(),
            P(),
            P(),
            P(),
            P(),
            P(),
            P(),
            P(),
            P(None, "ba"),
            P(None, "ba"),
            P(None, "ba"),
            P("ba", None),
        ),
        out_specs=P(("aa", "ba"), None),
        check_vma=False,
    )
```

profile of v0, /device:TPU:0, one launch (start us, length us, event | category | flops | bytes accessed | tf_op | source)
XLA Modules:
  0.0 332.6 jit_solution(549942878547130094)
XLA Ops:
  6.5 5.1 %collective-permute-start = (bf16[1,4,128,256]{3,2,1,0:T(8,128)(2,1)}, bf16[1,4,128,256]{3,2,1,0:T(8,128)(2,1)S(1)}, u32[]{:S(2)}, u32[]{:S(2)}) collective-permute-start(bf16[1,4,128,256]{3,2,1,0:T(8,128)(2,1)} %param.16), channel_id=1, source_target_pairs={{0,8},{8,16},{16,24},{1,9},{9,17},{17,25},{2,10},{10,18},{18,26},{... | collective-permute-start | bytes 786440 | tf_op jit(solution)/shard_map/ppermute | solution.py:18
  12.9 4.5 %collective-permute-done = bf16[1,4,128,256]{3,2,1,0:T(8,128)(2,1)S(1)} collective-permute-done((bf16[1,4,128,256]{3,2,1,0:T(8,128)(2,1)}, bf16[1,4,128,256]{3,2,1,0:T(8,128)(2,1)S(1)}, u32[]{:S(2)}, u32[]{:S(2)}) %collective-permute-start) | collective-permute-done | bytes 262176 | tf_op jit(solution)/shard_map/ppermute | solution.py:18
  18.5 3.0 collective-permute-done.1
  36.8 3.5 %collective-permute-start.4 = (bf16[1,4,128,256]{3,2,1,0:T(8,128)(2,1)S(1)}, bf16[1,4,128,256]{3,2,1,0:T(8,128)(2,1)S(1)}, u32[]{:S(2)}, u32[]{:S(2)}) collective-permute-start(bf16[1,4,128,256]{3,2,1,0:T(8,128)(2,1)S(1)} %fusion.66), channel_id=1, source_target_pairs={{0,8},{8,16},{16,24},{1,9},{9,17},{17,25},{2,10},{10,18},{18,26},{... | collective-permute-start | bytes 786440 | tf_op jit(solution)/shard_map/ppermute | solution.py:18
  44.1 4.4 %collective-permute-done.5 = bf16[1,4,128,256]{3,2,1,0:T(8,128)(2,1)S(1)} collective-permute-done((bf16[1,4,128,256]{3,2,1,0:T(8,128)(2,1)S(1)}, bf16[1,4,128,256]{3,2,1,0:T(8,128)(2,1)S(1)}, u32[]{:S(2)}, u32[]{:S(2)}) %collective-permute-start.5) | collective-permute-done | bytes 262176 | tf_op jit(solution)/shard_map/ppermute | solution.py:20
  49.3 5.3 %collective-permute-start.6 = (bf16[3,1,128,256]{3,2,1,0:T(8,128)(2,1)}, bf16[3,1,128,256]{3,2,1,0:T(8,128)(2,1)}, u32[]{:S(2)}, u32[]{:S(2)}) collective-permute-start(bf16[3,1,128,256]{3,2,1,0:T(8,128)(2,1)} %get-tuple-element.246), channel_id=1, source_target_pairs={{0,1},{1,2},{2,3},{3,4},{4,5},{5,6},{6,7},{8,9},{9,10},{10,11},{11... | collective-permute-start | bytes 589832 | tf_op jit(solution)/shard_map/ppermute | solution.py:18
  74.7 15.0 %all_gather.9 = bf16[1024,128]{1,0:T(8,128)(2,1)S(1)} all-gather(bf16[128,128]{1,0:T(8,128)(2,1)S(1)} %fusion.31), channel_id=1, replica_groups=mesh['aa'=4,'ba'=8] {'ba'}, dimensions={0}, use_global_device_ids=true | all-gather | bytes 294912 | tf_op jit(solution)/shard_map/all_gather | solution.py:134
  92.9 4.3 %fusion.25 = bf16[1024,768]{0,1:T(8,128)(2,1)S(1)} fusion(bf16[2048,256]{1,0:T(8,128)(2,1)S(1)} %copy-done.16, bf16[2048,256]{1,0:T(8,128)(2,1)S(1)} %copy-done.17, bf16[2048,256]{1,0:T(8,128)(2,1)S(1)} %copy-done.18, f32[1024,2048]{1,0:T(8,128)S(1)} %get-tuple-element.255, f32[2048]{0:T(1024)S(1)} %copy-done.19, f32[1024]{0:T(1024)S(1)} %add_rsqrt_fusion, ...), kind=kOutput, calls=%fused_computation.33 | convolution fusion | flops 3241934848 | bytes 13131776 | tf_op jit(solution)/shard_map/dot_general | solution.py:132
  99.4 43.0 %all-gather.3.cloned.1.call-done = bf16[4096,256]{0,1:T(8,128)(2,1)} async-done(((bf16[1024,256]{0,1:T(8,128)(2,1)}), bf16[4096,256]{0,1:T(8,128)(2,1)}) %all-gather.3.cloned.1.call-update) | async-done | bytes 2097168 | tf_op jit(solution)/shard_map/all_gather | solution.py:75
  142.4 46.1 %all-gather.5.cloned.1.call-done = bf16[4096,256]{0,1:T(8,128)(2,1)} async-done(((bf16[1024,256]{0,1:T(8,128)(2,1)}), bf16[4096,256]{0,1:T(8,128)(2,1)}) %all-gather.5.cloned.1.call-update) | async-done | bytes 2097168 | tf_op jit(solution)/shard_map/all_gather | solution.py:76
  188.4 101.7 %while.18 = (s32[]{:T(128)}, f32[4,1024]{1,0:T(4,128)S(1)}, f32[4,1024]{1,0:T(4,128)S(1)}, f32[1024,4,64]{0,2,1:T(8,128)S(1)}, bf16[4096,256]{0,1:T(8,128)(2,1)}...) while((s32[]{:T(128)}, f32[4,1024]{1,0:T(4,128)S(1)}, ...), condition=%wide.region_5.6_spmd.clone, body=%wide.region_2.5_spmd.clone.sunk | while | flops 1108107264 | bytes 56361128 | solution.py:104
  189.7 8.1 %bitcast_reduce_fusion.2 = (f32[4,1024]{1,0:T(4,128)S(1)}, f32[4,1024,1024]{2,1,0:T(8,128)}) fusion(bf16[1024,4,64]{0,2,1:T(8,128)(2,1)S(1)} %bitcast.131, bf16[1024,4,64]{0,2,1:T(8,128)(2,1)S(1)} %get-tuple-element.340), kind=kOutput, calls=%fused_computation.1.clone.1 | convolution fusion | flops 545255424 | bytes 17842176 | tf_op jit(solution)/shard_map/while/body/eval_jaxpr/qhd,khd->hqk/dot_general | solution.py:89
  197.9 7.4 %fusion.168 = f32[1024,4,64]{0,2,1:T(8,128)S(1)} fusion(bf16[1024,4,64]{0,2,1:T(8,128)(2,1)S(1)} %bitcast.132, f32[4,1024,1024]{2,1,0:T(8,128)} %get-tuple-element.310, f32[4,1024]{1,0:T(4,128)S(1)} %get-tuple-element.336, f32[1024,4,64]{0,2,1:T(8,128)S(1)} %get-tuple-element.327, f32[1024,4]{0,1:T(4,128)S(1)} %get-tuple-element.312, pred[]{:T(512)S(6)} %compare.43), kind=kOutput, calls=%fused_computation.7.clone.1 | convolution fusion | flops 550240256 | bytes 19431424 | tf_op jit(solution)/shard_map/while/body/eval_jaxpr/hqk,khd->qhd/dot_general | solution.py:96
  205.2 8.5 %fusion.166 = f32[4,1024]{1,0:T(4,128)S(1)} fusion(f32[4,1024,1024]{2,1,0:T(8,128)} %get-tuple-element.310, f32[4,1024]{1,0:T(4,128)S(1)} %get-tuple-element.336), kind=kLoop, calls=%fused_computation.4.clone.1 | loop fusion | flops 12578816 | bytes 16809984 | tf_op jit(solution)/shard_map/while/body/eval_jaxpr/reduce_sum | solution.py:95
  215.1 8.1 %bitcast_reduce_fusion.2 = (f32[4,1024]{1,0:T(4,128)S(1)}, f32[4,1024,1024]{2,1,0:T(8,128)}) fusion(bf16[1024,4,64]{0,2,1:T(8,128)(2,1)S(1)} %bitcast.131, bf16[1024,4,64]{0,2,1:T(8,128)(2,1)S(1)} %get-tuple-element.340), kind=kOutput, calls=%fused_computation.1.clone.1 | convolution fusion | flops 545255424 | bytes 17842176 | tf_op jit(solution)/shard_map/while/body/eval_jaxpr/qhd,khd->hqk/dot_general | solution.py:89
  223.3 7.4 %fusion.168 = f32[1024,4,64]{0,2,1:T(8,128)S(1)} fusion(bf16[1024,4,64]{0,2,1:T(8,128)(2,1)S(1)} %bitcast.132, f32[4,1024,1024]{2,1,0:T(8,128)} %get-tuple-element.310, f32[4,1024]{1,0:T(4,128)S(1)} %get-tuple-element.336, f32[1024,4,64]{0,2,1:T(8,128)S(1)} %get-tuple-element.327, f32[1024,4]{0,1:T(4,128)S(1)} %get-tuple-element.312, pred[]{:T(512)S(6)} %compare.43), kind=kOutput, calls=%fused_computation.7.clone.1 | convolution fusion | flops 550240256 | bytes 19431424 | tf_op jit(solution)/shard_map/while/body/eval_jaxpr/hqk,khd->qhd/dot_general | solution.py:96
  230.7 8.5 %fusion.166 = f32[4,1024]{1,0:T(4,128)S(1)} fusion(f32[4,1024,1024]{2,1,0:T(8,128)} %get-tuple-element.310, f32[4,1024]{1,0:T(4,128)S(1)} %get-tuple-element.336), kind=kLoop, calls=%fused_computation.4.clone.1 | loop fusion | flops 12578816 | bytes 16809984 | tf_op jit(solution)/shard_map/while/body/eval_jaxpr/reduce_sum | solution.py:95
  240.5 8.1 %bitcast_reduce_fusion.2 = (f32[4,1024]{1,0:T(4,128)S(1)}, f32[4,1024,1024]{2,1,0:T(8,128)}) fusion(bf16[1024,4,64]{0,2,1:T(8,128)(2,1)S(1)} %bitcast.131, bf16[1024,4,64]{0,2,1:T(8,128)(2,1)S(1)} %get-tuple-element.340), kind=kOutput, calls=%fused_computation.1.clone.1 | convolution fusion | flops 545255424 | bytes 17842176 | tf_op jit(solution)/shard_map/while/body/eval_jaxpr/qhd,khd->hqk/dot_general | solution.py:89
  248.7 7.4 %fusion.168 = f32[1024,4,64]{0,2,1:T(8,128)S(1)} fusion(bf16[1024,4,64]{0,2,1:T(8,128)(2,1)S(1)} %bitcast.132, f32[4,1024,1024]{2,1,0:T(8,128)} %get-tuple-element.310, f32[4,1024]{1,0:T(4,128)S(1)} %get-tuple-element.336, f32[1024,4,64]{0,2,1:T(8,128)S(1)} %get-tuple-element.327, f32[1024,4]{0,1:T(4,128)S(1)} %get-tuple-element.312, pred[]{:T(512)S(6)} %compare.43), kind=kOutput, calls=%fused_computation.7.clone.1 | convolution fusion | flops 550240256 | bytes 19431424 | tf_op jit(solution)/shard_map/while/body/eval_jaxpr/hqk,khd->qhd/dot_general | solution.py:96
  256.1 8.5 %fusion.166 = f32[4,1024]{1,0:T(4,128)S(1)} fusion(f32[4,1024,1024]{2,1,0:T(8,128)} %get-tuple-element.310, f32[4,1024]{1,0:T(4,128)S(1)} %get-tuple-element.336), kind=kLoop, calls=%fused_computation.4.clone.1 | loop fusion | flops 12578816 | bytes 16809984 | tf_op jit(solution)/shard_map/while/body/eval_jaxpr/reduce_sum | solution.py:95
  266.0 8.1 %bitcast_reduce_fusion.2 = (f32[4,1024]{1,0:T(4,128)S(1)}, f32[4,1024,1024]{2,1,0:T(8,128)}) fusion(bf16[1024,4,64]{0,2,1:T(8,128)(2,1)S(1)} %bitcast.131, bf16[1024,4,64]{0,2,1:T(8,128)(2,1)S(1)} %get-tuple-element.340), kind=kOutput, calls=%fused_computation.1.clone.1 | convolution fusion | flops 545255424 | bytes 17842176 | tf_op jit(solution)/shard_map/while/body/eval_jaxpr/qhd,khd->hqk/dot_general | solution.py:89
  274.1 7.4 %fusion.168 = f32[1024,4,64]{0,2,1:T(8,128)S(1)} fusion(bf16[1024,4,64]{0,2,1:T(8,128)(2,1)S(1)} %bitcast.132, f32[4,1024,1024]{2,1,0:T(8,128)} %get-tuple-element.310, f32[4,1024]{1,0:T(4,128)S(1)} %get-tuple-element.336, f32[1024,4,64]{0,2,1:T(8,128)S(1)} %get-tuple-element.327, f32[1024,4]{0,1:T(4,128)S(1)} %get-tuple-element.312, pred[]{:T(512)S(6)} %compare.43), kind=kOutput, calls=%fused_computation.7.clone.1 | convolution fusion | flops 550240256 | bytes 19431424 | tf_op jit(solution)/shard_map/while/body/eval_jaxpr/hqk,khd->qhd/dot_general | solution.py:96
  281.5 8.5 %fusion.166 = f32[4,1024]{1,0:T(4,128)S(1)} fusion(f32[4,1024,1024]{2,1,0:T(8,128)} %get-tuple-element.310, f32[4,1024]{1,0:T(4,128)S(1)} %get-tuple-element.336), kind=kLoop, calls=%fused_computation.4.clone.1 | loop fusion | flops 12578816 | bytes 16809984 | tf_op jit(solution)/shard_map/while/body/eval_jaxpr/reduce_sum | solution.py:95
  292.0 32.6 %reduce-scatter.2.cloned.1.call-done = bf16[128,128]{1,0:T(8,128)(2,1)} async-done(((bf16[1024,128]{1,0:T(8,128)(2,1)}), bf16[128,128]{1,0:T(8,128)(2,1)}) %reduce-scatter.2.cloned.1.call-update) | async-done | bytes 32784 | tf_op jit(solution)/shard_map/reduce_scatter | solution.py:140
  (132 shorter events, 55.6 us)
Async XLA Ops:
  6.5 83.1 %copy-start = (bf16[128,2048]{1,0:T(8,128)(2,1)S(1)}, bf16[128,2048]{1,0:T(8,128)(2,1)}, u32[]{:S(2)}) copy-start(bf16[128,2048]{1,0:T(8,128)(2,1)} %param.23) | copy-start | bytes 1572868
  6.5 135.8 %all-gather.3.cloned.1.call-start = ((), (), s32[]{:S(2)}) async-start(), calls=%async_computation.1 | async-start | bytes 2621440 | tf_op jit(solution)/shard_map/all_gather | solution.py:75
  6.5 10.9 %collective-permute-start = (bf16[1,4,128,256]{3,2,1,0:T(8,128)(2,1)}, bf16[1,4,128,256]{3,2,1,0:T(8,128)(2,1)S(1)}, u32[]{:S(2)}, u32[]{:S(2)}) collective-permute-start(bf16[1,4,128,256]{3,2,1,0:T(8,128)(2,1)} %param.16), channel_id=1, source_target_pairs={{0,8},{8,16},{16,24},{1,9},{9,17},{17,25},{2,10},{10,18},{18,26},{... | collective-permute-start | bytes 786440 | tf_op jit(solution)/shard_map/ppermute | solution.py:18
  11.6 9.9 %collective-permute-start.1 = (bf16[1,4,128,256]{3,2,1,0:T(8,128)(2,1)}, bf16[1,4,128,256]{3,2,1,0:T(8,128)(2,1)S(1)}, u32[]{:S(2)}, u32[]{:S(2)}) collective-permute-start(bf16[1,4,128,256]{3,2,1,0:T(8,128)(2,1)} %param.16), channel_id=1, source_target_pairs={{8,0},{16,8},{24,16},{9,1},{17,9},{25,17},{10,2},{18,10},{26,18},{... | collective-permute-start | bytes 786440 | tf_op jit(solution)/shard_map/ppermute | solution.py:20
  21.6 4.8 %collective-permute-start.2 = (bf16[3,1,128,256]{3,2,1,0:T(8,128)(2,1)S(1)}, bf16[3,1,128,256]{3,2,1,0:T(8,128)(2,1)S(1)}, u32[]{:S(2)}, u32[]{:S(2)}) collective-permute-start(bf16[3,1,128,256]{3,2,1,0:T(8,128)(2,1)S(1)} %get-tuple-element.248), channel_id=1, source_target_pairs={{0,1},{1,2},{2,3},{3,4},{4,5},{5,6},{6,7},{8,9},{9,10},{10,11},{11... | collective-permute-start | bytes 589832 | tf_op jit(solution)/shard_map/ppermute | solution.py:18
  22.9 5.1 %collective-permute-start.3 = (bf16[3,1,128,256]{3,2,1,0:T(8,128)(2,1)S(1)}, bf16[3,1,128,256]{3,2,1,0:T(8,128)(2,1)S(1)}, u32[]{:S(2)}, u32[]{:S(2)}) collective-permute-start(bf16[3,1,128,256]{3,2,1,0:T(8,128)(2,1)S(1)} %get-tuple-element.247), channel_id=1, source_target_pairs={{1,0},{2,1},{3,2},{4,3},{5,4},{6,5},{7,6},{9,8},{10,9},{11,10},{12... | collective-permute-start | bytes 589832 | tf_op jit(solution)/shard_map/ppermute | solution.py:20
  33.6 22.5 %copy-start.2 = (bf16[3,3,3,256,256]{4,3,2,1,0:T(8,128)(2,1)S(1)}, bf16[3,3,3,256,256]{4,3,2,1,0:T(8,128)(2,1)}, u32[]{:S(2)}) copy-start(bf16[3,3,3,256,256]{4,3,2,1,0:T(8,128)(2,1)} %param.19) | copy-start | bytes 10616836
  36.8 7.3 %collective-permute-start.4 = (bf16[1,4,128,256]{3,2,1,0:T(8,128)(2,1)S(1)}, bf16[1,4,128,256]{3,2,1,0:T(8,128)(2,1)S(1)}, u32[]{:S(2)}, u32[]{:S(2)}) collective-permute-start(bf16[1,4,128,256]{3,2,1,0:T(8,128)(2,1)S(1)} %fusion.66), channel_id=1, source_target_pairs={{0,8},{8,16},{16,24},{1,9},{9,17},{17,25},{2,10},{10,18},{18,26},{... | collective-permute-start | bytes 786440 | tf_op jit(solution)/shard_map/ppermute | solution.py:18
  40.3 8.3 %collective-permute-start.5 = (bf16[1,4,128,256]{3,2,1,0:T(8,128)(2,1)S(1)}, bf16[1,4,128,256]{3,2,1,0:T(8,128)(2,1)S(1)}, u32[]{:S(2)}, u32[]{:S(2)}) collective-permute-start(bf16[1,4,128,256]{3,2,1,0:T(8,128)(2,1)S(1)} %fusion.66), channel_id=1, source_target_pairs={{8,0},{16,8},{24,16},{9,1},{17,9},{25,17},{10,2},{18,10},{26,18},{... | collective-permute-start | bytes 786440 | tf_op jit(solution)/shard_map/ppermute | solution.py:20
  49.3 9.1 %collective-permute-start.6 = (bf16[3,1,128,256]{3,2,1,0:T(8,128)(2,1)}, bf16[3,1,128,256]{3,2,1,0:T(8,128)(2,1)}, u32[]{:S(2)}, u32[]{:S(2)}) collective-permute-start(bf16[3,1,128,256]{3,2,1,0:T(8,128)(2,1)} %get-tuple-element.246), channel_id=1, source_target_pairs={{0,1},{1,2},{2,3},{3,4},{4,5},{5,6},{6,7},{8,9},{9,10},{10,11},{11... | collective-permute-start | bytes 589832 | tf_op jit(solution)/shard_map/ppermute | solution.py:18
  54.6 5.0 %collective-permute-start.7 = (bf16[3,1,128,256]{3,2,1,0:T(8,128)(2,1)}, bf16[3,1,128,256]{3,2,1,0:T(8,128)(2,1)S(1)}, u32[]{:S(2)}, u32[]{:S(2)}) collective-permute-start(bf16[3,1,128,256]{3,2,1,0:T(8,128)(2,1)} %get-tuple-element.245), channel_id=1, source_target_pairs={{1,0},{2,1},{3,2},{4,3},{5,4},{6,5},{7,6},{9,8},{10,9},{11,10},{12... | collective-permute-start | bytes 589832 | tf_op jit(solution)/shard_map/ppermute | solution.py:20
  62.0 1.1 copy-start.9
  64.8 1.1 copy-start.6
  65.9 1.1 copy-start.21
  66.3 1.1 copy-start.5
  70.8 2.7 copy-start.15
  70.8 18.9 %copy-start.12 = (f32[2048]{0:T(1024)S(1)}, f32[2048]{0:T(1024)}, u32[]{:S(2)}) copy-start(f32[2048]{0:T(1024)} %param.24) | copy-start | bytes 24580
  91.0 1.3 copy-start.16
  91.0 1.5 copy-start.17
  91.0 1.8 copy-start.18
  91.0 1.8 copy-start.19
  98.3 90.1 %all-gather.5.cloned.1.call-start = ((), (), s32[]{:S(2)}) async-start(), calls=%async_computation.2 | async-start | bytes 2621440 | tf_op jit(solution)/shard_map/all_gather | solution.py:76
  99.1 225.6 %reduce-scatter.2.cloned.1.call-start = ((), (), s32[]{:S(2)}) async-start(), calls=%async_computation.3 | async-start | bytes 294912 | tf_op jit(solution)/shard_map/reduce_scatter | solution.py:140
  290.1 35.9 %copy-start.1 = (bf16[128,2048]{1,0:T(8,128)(2,1)S(1)}, bf16[128,2048]{1,0:T(8,128)(2,1)}, u32[]{:S(2)}) copy-start(bf16[128,2048]{1,0:T(8,128)(2,1)} %param.23) | copy-start | bytes 1572868
  (9 other events, 8.5 us)
Sparse Core Ops, SparseCore 0:
  98.4 43.8 all-gather.2
  143.9 44.4 all-gather.4
  292.1 32.4 reduce-scatter.1
where the time goes:
time: 334 us; the launch traced here: 333 us
  waiting for transfers between devices  140 us (42%)
  matrix products  78.4 us (23%)
  other arithmetic  45.5 us (14%)
  starting transfers between devices  20.9 us (6%)
  local copies, waits for them, and re-layouts  19.1 us (6%)
  blocking collectives  15 us (4%)
  between operations  13.7 us (4%)
    all_gather x1, waiting for transfers between devices, attend(): value_rows = lax.all_gather(values, 'aa', axis=0, tiled=True)  46.1 us
    all_gather x1, waiting for transfers between devices, attend(): key_rows = lax.all_gather(keys, 'aa', axis=0, tiled=True)  43 us
    reduce_sum x4, other arithmetic, one_step(): denom = denom * fade + probs.sum(-1)  34.1 us
    reduce_scatter x1, waiting for transfers between devices, on_device(): lax.psum_scatter(jnp.dot(attended, w_velocity, preferred_element_type=jnp...  32.6 us
    dot_general x4, matrix products, one_step(): jnp.einsum('qhd,khd->hqk', query_heads, key_block, preferred_element_type...  32.6 us
    dot_general x4, matrix products, one_step(): jnp.einsum('hqk,khd->qhd', probs.astype(jnp.bfloat16), value_block, prefe...  29.5 us
    ppermute x4, starting transfers between devices, with_halo(): lax.ppermute(tail, axis, [(i, (i + 1) % count) for i in range(ends)])  15.2 us
    all_gather x1, blocking collectives, on_device(): lax.all_gather(latents, 'ba', axis=0, tiled=True)  15 us
  transfers between devices with their start and end apart: 11, of which 9 were waited for; matrix products, arithmetic and copies ran while one was open for 2% of the time, Pallas kernels for 0%

commit v1 on v0

--- a/solution.py
+++ b/solution.py
@@ -73,7 +73,11 @@
         jnp.zeros((rows, heads, HEAD_DIM), jnp.float32),
     )
     key_rows = lax.all_gather(keys, "aa", axis=0, tiled=True)
-    value_rows = lax.all_gather(values, "aa", axis=0, tiled=True)
+    size = lax.axis_size("aa")
+    repeats = [size if d == 0 else 1 for d in range(values.ndim)]
+    value_rows = lax.all_to_all(
+        jnp.tile(values, repeats), "aa", split_axis=0, concat_axis=0, tiled=True
+    )
     count = key_rows.shape[0]
     block = math.gcd(count, 1024)
 

time: 334 us -> 339 us (1.015)
  local copies, waits for them, and re-layouts: 19.1 us -> 28.9 us
  waiting for transfers between devices: 140 us -> 131 us
  starting transfers between devices: 20.9 us -> 25.3 us
    all_to_all x0 -> x1, waiting for transfers between devices: none -> 81.7 us  [attend(): lax.all_to_all(jnp.tile(values, repeats), 'aa', split_axis=0, concat_axis...]
    all_gather x1 -> x0, waiting for transfers between devices: 46.1 us -> none  [attend(): value_rows = lax.all_gather(values, 'aa', axis=0, tiled=True)]
    all_gather x1, waiting for transfers between devices: 43 us -> 0.01 us  [attend(): key_rows = lax.all_gather(keys, 'aa', axis=0, tiled=True)]
    all_to_all x0 -> x1, starting transfers between devices: none -> 4.43 us  [attend(): lax.all_to_all(jnp.tile(values, repeats), 'aa', split_axis=0, concat_axis...]
    dynamic_slice x0 -> x4, local copies, waits for them, and re-layouts: none -> 4.32 us  [one_step(): lax.dynamic_slice_in_dim(key_rows, index * block, block, 0)]
    all_to_all x0 -> x1, local copies, waits for them, and re-layouts: none -> 3.95 us  [attend(): lax.all_to_all(jnp.tile(values, repeats), 'aa', split_axis=0, concat_axis...]
  transfers between devices with their start and end apart: 11 -> 11, of which waited for: 9 -> 8; matrix products, arithmetic and copies ran while one was open for 2% -> 3% of each run, Pallas kernels for 0% -> 0%
where the time goes in v1:
time: 339 us; the launch traced here: 337 us
  waiting for transfers between devices  131 us (39%)
  matrix products  77.5 us (23%)
  other arithmetic  45.4 us (13%)
  local copies, waits for them, and re-layouts  28.9 us (9%)
  starting transfers between devices  25.3 us (7%)
  blocking collectives  15 us (4%)
  between operations  14.1 us (4%)
    all_to_all x1, waiting for transfers between devices, attend(): lax.all_to_all(jnp.tile(values, repeats), 'aa', split_axis=0, concat_axis...  81.7 us
    reduce_sum x4, other arithmetic, one_step(): denom = denom * fade + probs.sum(-1)  34 us
    dot_general x4, matrix products, one_step(): jnp.einsum('qhd,khd->hqk', query_heads, key_block, preferred_element_type...  32.6 us
    reduce_scatter x1, waiting for transfers between devices, on_device(): lax.psum_scatter(jnp.dot(attended, w_velocity, preferred_element_type=jnp...  31.1 us
    dot_general x4, matrix products, one_step(): jnp.einsum('hqk,khd->qhd', probs.astype(jnp.bfloat16), value_block, prefe...  29.5 us
    ppermute x4, starting transfers between devices, with_halo(): lax.ppermute(tail, axis, [(i, (i + 1) % count) for i in range(ends)])  15.2 us
    all_gather x1, blocking collectives, on_device(): lax.all_gather(latents, 'ba', axis=0, tiled=True)  15 us
    ppermute x4, waiting for transfers between devices, with_halo(): lax.ppermute(head, axis, [((i + 1) % count, i) for i in range(ends)])  10.3 us
  transfers between devices with their start and end apart: 11, of which 8 were waited for; matrix products, arithmetic and copies ran while one was open for 3% of the time, Pallas kernels for 0%

profile of v1, /device:TPU:0, one launch (start us, length us, event | category | flops | bytes accessed | tf_op | source)
XLA Modules:
  0.0 337.2 jit_solution(13064511340146854821)
XLA Ops:
  6.5 5.1 %collective-permute-start = (bf16[1,4,128,256]{3,2,1,0:T(8,128)(2,1)}, bf16[1,4,128,256]{3,2,1,0:T(8,128)(2,1)S(1)}, u32[]{:S(2)}, u32[]{:S(2)}) collective-permute-start(bf16[1,4,128,256]{3,2,1,0:T(8,128)(2,1)} %param.16), channel_id=1, source_target_pairs={{0,8},{8,16},{16,24},{1,9},{9,17},{17,25},{2,10},{10,18},{18,26},{... | collective-permute-start | bytes 786440 | tf_op jit(solution)/shard_map/ppermute | solution.py:18
  12.9 4.5 %collective-permute-done = bf16[1,4,128,256]{3,2,1,0:T(8,128)(2,1)S(1)} collective-permute-done((bf16[1,4,128,256]{3,2,1,0:T(8,128)(2,1)}, bf16[1,4,128,256]{3,2,1,0:T(8,128)(2,1)S(1)}, u32[]{:S(2)}, u32[]{:S(2)}) %collective-permute-start) | collective-permute-done | bytes 262176 | tf_op jit(solution)/shard_map/ppermute | solution.py:18
  36.8 3.5 %collective-permute-start.4 = (bf16[1,4,128,256]{3,2,1,0:T(8,128)(2,1)S(1)}, bf16[1,4,128,256]{3,2,1,0:T(8,128)(2,1)S(1)}, u32[]{:S(2)}, u32[]{:S(2)}) collective-permute-start(bf16[1,4,128,256]{3,2,1,0:T(8,128)(2,1)S(1)} %fusion.66), channel_id=1, source_target_pairs={{0,8},{8,16},{16,24},{1,9},{9,17},{17,25},{2,10},{10,18},{18,26},{... | collective-permute-start | bytes 786440 | tf_op jit(solution)/shard_map/ppermute | solution.py:18
  44.2 4.4 %collective-permute-done.5 = bf16[1,4,128,256]{3,2,1,0:T(8,128)(2,1)S(1)} collective-permute-done((bf16[1,4,128,256]{3,2,1,0:T(8,128)(2,1)S(1)}, bf16[1,4,128,256]{3,2,1,0:T(8,128)(2,1)S(1)}, u32[]{:S(2)}, u32[]{:S(2)}) %collective-permute-start.5) | collective-permute-done | bytes 262176 | tf_op jit(solution)/shard_map/ppermute | solution.py:20
  49.3 5.3 %collective-permute-start.6 = (bf16[3,1,128,256]{3,2,1,0:T(8,128)(2,1)}, bf16[3,1,128,256]{3,2,1,0:T(8,128)(2,1)}, u32[]{:S(2)}, u32[]{:S(2)}) collective-permute-start(bf16[3,1,128,256]{3,2,1,0:T(8,128)(2,1)} %get-tuple-element.265), channel_id=1, source_target_pairs={{0,1},{1,2},{2,3},{3,4},{4,5},{5,6},{6,7},{8,9},{9,10},{10,11},{11... | collective-permute-start | bytes 589832 | tf_op jit(solution)/shard_map/ppermute | solution.py:18
  73.8 15.0 %all_gather.6 = bf16[1024,128]{1,0:T(8,128)(2,1)S(1)} all-gather(bf16[128,128]{1,0:T(8,128)(2,1)S(1)} %fusion.31), channel_id=1, replica_groups=mesh['aa'=4,'ba'=8] {'ba'}, dimensions={0}, use_global_device_ids=true | all-gather | bytes 294912 | tf_op jit(solution)/shard_map/all_gather | solution.py:138
  92.0 4.3 %fusion.25 = bf16[1024,768]{0,1:T(8,128)(2,1)S(1)} fusion(bf16[2048,256]{1,0:T(8,128)(2,1)S(1)} %copy-done.17, bf16[2048,256]{1,0:T(8,128)(2,1)S(1)} %copy-done.18, bf16[2048,256]{1,0:T(8,128)(2,1)S(1)} %copy-done.19, f32[1024,2048]{1,0:T(8,128)S(1)} %get-tuple-element.274, f32[2048]{0:T(1024)S(1)} %copy-done.20, f32[1024]{0:T(1024)S(1)} %add_rsqrt_fusion, ...), kind=kOutput, calls=%fused_computation.33 | convolution fusion | flops 3241934848 | bytes 13131776 | tf_op jit(solution)/shard_map/dot_general | solution.py:136
  98.8 4.4 %all-to-all-start = ((bf16[4,1024,256]{1,2,0:T(8,128)(2,1)}), bf16[4,1024,256]{1,2,0:T(8,128)(2,1)}, u32[]{:S(2)}, u32[]{:S(2)}) async-start(bf16[4,1024,256]{1,2,0:T(8,128)(2,1)} %tile.2), calls=%async_computation | async-start | bytes 4194304 | tf_op jit(solution)/shard_map/all_to_all | solution.py:78
  104.3 81.7 %all-to-all-done = bf16[4,1024,256]{1,2,0:T(8,128)(2,1)} async-done(((bf16[4,1024,256]{1,2,0:T(8,128)(2,1)}), bf16[4,1024,256]{1,2,0:T(8,128)(2,1)}, u32[]{:S(2)}, u32[]{:S(2)}) %all-to-all-start) | async-done | bytes 2097184 | tf_op jit(solution)/shard_map/all_to_all | solution.py:78
  186.0 3.9 %copy.75 = bf16[4,1024,256]{2,1,0:T(8,128)(2,1)} copy(bf16[4,1024,256]{1,2,0:T(8,128)(2,1)} %all-to-all-done) | data formatting | bytes 4194304 | tf_op jit(solution)/shard_map/all_to_all | solution.py:78
  190.0 106.0 %while.18 = (s32[]{:T(128)}, f32[4,1024]{1,0:T(4,128)S(1)}, f32[4,1024]{1,0:T(4,128)S(1)}, f32[1024,4,64]{0,2,1:T(8,128)S(1)}, bf16[4096,256]{0,1:T(8,128)(2,1)}...) while((s32[]{:T(128)}, f32[4,1024]{1,0:T(4,128)S(1)}, ...), condition=%wide.region_5.6_spmd.clone, body=%wide.region_2.5_spmd.clone.sunk | while | flops 1108107264 | bytes 57409708 | solution.py:108
  191.1 8.1 %bitcast_reduce_fusion.2 = (f32[4,1024]{1,0:T(4,128)S(1)}, f32[4,1024,1024]{2,1,0:T(8,128)}) fusion(bf16[1024,4,64]{0,2,1:T(8,128)(2,1)S(1)} %bitcast.132, bf16[1024,4,64]{0,2,1:T(8,128)(2,1)S(1)} %get-tuple-element.355), kind=kOutput, calls=%fused_computation.1.clone.1 | convolution fusion | flops 545255424 | bytes 17842176 | tf_op jit(solution)/shard_map/while/body/eval_jaxpr/qhd,khd->hqk/dot_general | solution.py:93
  200.5 7.4 %fusion.168 = f32[1024,4,64]{0,2,1:T(8,128)S(1)} fusion(bf16[1024,4,64]{0,2,1:T(8,128)(2,1)S(1)} %bitcast.133, f32[4,1024,1024]{2,1,0:T(8,128)} %get-tuple-element.326, f32[4,1024]{1,0:T(4,128)S(1)} %get-tuple-element.351, f32[1024,4,64]{0,2,1:T(8,128)S(1)} %get-tuple-element.342, f32[1024,4]{0,1:T(4,128)S(1)} %get-tuple-element.327, pred[]{:T(512)S(6)} %compare.43), kind=kOutput, calls=%fused_computation.7.clone.1 | convolution fusion | flops 550240256 | bytes 19431424 | tf_op jit(solution)/shard_map/while/body/eval_jaxpr/hqk,khd->qhd/dot_general | solution.py:100
  207.9 8.5 %fusion.166 = f32[4,1024]{1,0:T(4,128)S(1)} fusion(f32[4,1024,1024]{2,1,0:T(8,128)} %get-tuple-element.326, f32[4,1024]{1,0:T(4,128)S(1)} %get-tuple-element.351), kind=kLoop, calls=%fused_computation.4.clone.1 | loop fusion | flops 12578816 | bytes 16809984 | tf_op jit(solution)/shard_map/while/body/eval_jaxpr/reduce_sum | solution.py:99
  217.6 8.1 %bitcast_reduce_fusion.2 = (f32[4,1024]{1,0:T(4,128)S(1)}, f32[4,1024,1024]{2,1,0:T(8,128)}) fusion(bf16[1024,4,64]{0,2,1:T(8,128)(2,1)S(1)} %bitcast.132, bf16[1024,4,64]{0,2,1:T(8,128)(2,1)S(1)} %get-tuple-element.355), kind=kOutput, calls=%fused_computation.1.clone.1 | convolution fusion | flops 545255424 | bytes 17842176 | tf_op jit(solution)/shard_map/while/body/eval_jaxpr/qhd,khd->hqk/dot_general | solution.py:93
  227.0 7.4 %fusion.168 = f32[1024,4,64]{0,2,1:T(8,128)S(1)} fusion(bf16[1024,4,64]{0,2,1:T(8,128)(2,1)S(1)} %bitcast.133, f32[4,1024,1024]{2,1,0:T(8,128)} %get-tuple-element.326, f32[4,1024]{1,0:T(4,128)S(1)} %get-tuple-element.351, f32[1024,4,64]{0,2,1:T(8,128)S(1)} %get-tuple-element.342, f32[1024,4]{0,1:T(4,128)S(1)} %get-tuple-element.327, pred[]{:T(512)S(6)} %compare.43), kind=kOutput, calls=%fused_computation.7.clone.1 | convolution fusion | flops 550240256 | bytes 19431424 | tf_op jit(solution)/shard_map/while/body/eval_jaxpr/hqk,khd->qhd/dot_general | solution.py:100
  234.4 8.5 %fusion.166 = f32[4,1024]{1,0:T(4,128)S(1)} fusion(f32[4,1024,1024]{2,1,0:T(8,128)} %get-tuple-element.326, f32[4,1024]{1,0:T(4,128)S(1)} %get-tuple-element.351), kind=kLoop, calls=%fused_computation.4.clone.1 | loop fusion | flops 12578816 | bytes 16809984 | tf_op jit(solution)/shard_map/while/body/eval_jaxpr/reduce_sum | solution.py:99
  244.1 8.1 %bitcast_reduce_fusion.2 = (f32[4,1024]{1,0:T(4,128)S(1)}, f32[4,1024,1024]{2,1,0:T(8,128)}) fusion(bf16[1024,4,64]{0,2,1:T(8,128)(2,1)S(1)} %bitcast.132, bf16[1024,4,64]{0,2,1:T(8,128)(2,1)S(1)} %get-tuple-element.355), kind=kOutput, calls=%fused_computation.1.clone.1 | convolution fusion | flops 545255424 | bytes 17842176 | tf_op jit(solution)/shard_map/while/body/eval_jaxpr/qhd,khd->hqk/dot_general | solution.py:93
  253.5 7.4 %fusion.168 = f32[1024,4,64]{0,2,1:T(8,128)S(1)} fusion(bf16[1024,4,64]{0,2,1:T(8,128)(2,1)S(1)} %bitcast.133, f32[4,1024,1024]{2,1,0:T(8,128)} %get-tuple-element.326, f32[4,1024]{1,0:T(4,128)S(1)} %get-tuple-element.351, f32[1024,4,64]{0,2,1:T(8,128)S(1)} %get-tuple-element.342, f32[1024,4]{0,1:T(4,128)S(1)} %get-tuple-element.327, pred[]{:T(512)S(6)} %compare.43), kind=kOutput, calls=%fused_computation.7.clone.1 | convolution fusion | flops 550240256 | bytes 19431424 | tf_op jit(solution)/shard_map/while/body/eval_jaxpr/hqk,khd->qhd/dot_general | solution.py:100
  260.9 8.5 %fusion.166 = f32[4,1024]{1,0:T(4,128)S(1)} fusion(f32[4,1024,1024]{2,1,0:T(8,128)} %get-tuple-element.326, f32[4,1024]{1,0:T(4,128)S(1)} %get-tuple-element.351), kind=kLoop, calls=%fused_computation.4.clone.1 | loop fusion | flops 12578816 | bytes 16809984 | tf_op jit(solution)/shard_map/while/body/eval_jaxpr/reduce_sum | solution.py:99
  270.6 8.1 %bitcast_reduce_fusion.2 = (f32[4,1024]{1,0:T(4,128)S(1)}, f32[4,1024,1024]{2,1,0:T(8,128)}) fusion(bf16[1024,4,64]{0,2,1:T(8,128)(2,1)S(1)} %bitcast.132, bf16[1024,4,64]{0,2,1:T(8,128)(2,1)S(1)} %get-tuple-element.355), kind=kOutput, calls=%fused_computation.1.clone.1 | convolution fusion | flops 545255424 | bytes 17842176 | tf_op jit(solution)/shard_map/while/body/eval_jaxpr/qhd,khd->hqk/dot_general | solution.py:93
  280.0 7.4 %fusion.168 = f32[1024,4,64]{0,2,1:T(8,128)S(1)} fusion(bf16[1024,4,64]{0,2,1:T(8,128)(2,1)S(1)} %bitcast.133, f32[4,1024,1024]{2,1,0:T(8,128)} %get-tuple-element.326, f32[4,1024]{1,0:T(4,128)S(1)} %get-tuple-element.351, f32[1024,4,64]{0,2,1:T(8,128)S(1)} %get-tuple-element.342, f32[1024,4]{0,1:T(4,128)S(1)} %get-tuple-element.327, pred[]{:T(512)S(6)} %compare.43), kind=kOutput, calls=%fused_computation.7.clone.1 | convolution fusion | flops 550240256 | bytes 19431424 | tf_op jit(solution)/shard_map/while/body/eval_jaxpr/hqk,khd->qhd/dot_general | solution.py:100
  287.4 8.5 %fusion.166 = f32[4,1024]{1,0:T(4,128)S(1)} fusion(f32[4,1024,1024]{2,1,0:T(8,128)} %get-tuple-element.326, f32[4,1024]{1,0:T(4,128)S(1)} %get-tuple-element.351), kind=kLoop, calls=%fused_computation.4.clone.1 | loop fusion | flops 12578816 | bytes 16809984 | tf_op jit(solution)/shard_map/while/body/eval_jaxpr/reduce_sum | solution.py:99
  297.9 31.1 %reduce-scatter.2.cloned.1.call-done = bf16[128,128]{1,0:T(8,128)(2,1)} async-done(((bf16[1024,128]{1,0:T(8,128)(2,1)}), bf16[128,128]{1,0:T(8,128)(2,1)}) %reduce-scatter.2.cloned.1.call-update) | async-done | bytes 32784 | tf_op jit(solution)/shard_map/reduce_scatter | solution.py:144
  (143 shorter events, 63.6 us)
Async XLA Ops:
  6.5 82.2 %copy-start = (bf16[128,2048]{1,0:T(8,128)(2,1)S(1)}, bf16[128,2048]{1,0:T(8,128)(2,1)}, u32[]{:S(2)}) copy-start(bf16[128,2048]{1,0:T(8,128)(2,1)} %param.23) | copy-start | bytes 1572868
  6.5 10.9 %collective-permute-start = (bf16[1,4,128,256]{3,2,1,0:T(8,128)(2,1)}, bf16[1,4,128,256]{3,2,1,0:T(8,128)(2,1)S(1)}, u32[]{:S(2)}, u32[]{:S(2)}) collective-permute-start(bf16[1,4,128,256]{3,2,1,0:T(8,128)(2,1)} %param.16), channel_id=1, source_target_pairs={{0,8},{8,16},{16,24},{1,9},{9,17},{17,25},{2,10},{10,18},{18,26},{... | collective-permute-start | bytes 786440 | tf_op jit(solution)/shard_map/ppermute | solution.py:18
  11.6 9.9 %collective-permute-start.1 = (bf16[1,4,128,256]{3,2,1,0:T(8,128)(2,1)}, bf16[1,4,128,256]{3,2,1,0:T(8,128)(2,1)S(1)}, u32[]{:S(2)}, u32[]{:S(2)}) collective-permute-start(bf16[1,4,128,256]{3,2,1,0:T(8,128)(2,1)} %param.16), channel_id=1, source_target_pairs={{8,0},{16,8},{24,16},{9,1},{17,9},{25,17},{10,2},{18,10},{26,18},{... | collective-permute-start | bytes 786440 | tf_op jit(solution)/shard_map/ppermute | solution.py:20
  21.6 4.8 %collective-permute-start.2 = (bf16[3,1,128,256]{3,2,1,0:T(8,128)(2,1)S(1)}, bf16[3,1,128,256]{3,2,1,0:T(8,128)(2,1)S(1)}, u32[]{:S(2)}, u32[]{:S(2)}) collective-permute-start(bf16[3,1,128,256]{3,2,1,0:T(8,128)(2,1)S(1)} %get-tuple-element.267), channel_id=1, source_target_pairs={{0,1},{1,2},{2,3},{3,4},{4,5},{5,6},{6,7},{8,9},{9,10},{10,11},{11... | collective-permute-start | bytes 589832 | tf_op jit(solution)/shard_map/ppermute | solution.py:18
  22.9 5.1 %collective-permute-start.3 = (bf16[3,1,128,256]{3,2,1,0:T(8,128)(2,1)S(1)}, bf16[3,1,128,256]{3,2,1,0:T(8,128)(2,1)S(1)}, u32[]{:S(2)}, u32[]{:S(2)}) collective-permute-start(bf16[3,1,128,256]{3,2,1,0:T(8,128)(2,1)S(1)} %get-tuple-element.266), channel_id=1, source_target_pairs={{1,0},{2,1},{3,2},{4,3},{5,4},{6,5},{7,6},{9,8},{10,9},{11,10},{12... | collective-permute-start | bytes 589832 | tf_op jit(solution)/shard_map/ppermute | solution.py:20
  33.6 22.5 %copy-start.2 = (bf16[3,3,3,256,256]{4,3,2,1,0:T(8,128)(2,1)S(1)}, bf16[3,3,3,256,256]{4,3,2,1,0:T(8,128)(2,1)}, u32[]{:S(2)}) copy-start(bf16[3,3,3,256,256]{4,3,2,1,0:T(8,128)(2,1)} %param.19) | copy-start | bytes 10616836
  36.8 7.3 %collective-permute-start.4 = (bf16[1,4,128,256]{3,2,1,0:T(8,128)(2,1)S(1)}, bf16[1,4,128,256]{3,2,1,0:T(8,128)(2,1)S(1)}, u32[]{:S(2)}, u32[]{:S(2)}) collective-permute-start(bf16[1,4,128,256]{3,2,1,0:T(8,128)(2,1)S(1)} %fusion.66), channel_id=1, source_target_pairs={{0,8},{8,16},{16,24},{1,9},{9,17},{17,25},{2,10},{10,18},{18,26},{... | collective-permute-start | bytes 786440 | tf_op jit(solution)/shard_map/ppermute | solution.py:18
  40.3 8.3 %collective-permute-start.5 = (bf16[1,4,128,256]{3,2,1,0:T(8,128)(2,1)S(1)}, bf16[1,4,128,256]{3,2,1,0:T(8,128)(2,1)S(1)}, u32[]{:S(2)}, u32[]{:S(2)}) collective-permute-start(bf16[1,4,128,256]{3,2,1,0:T(8,128)(2,1)S(1)} %fusion.66), channel_id=1, source_target_pairs={{8,0},{16,8},{24,16},{9,1},{17,9},{25,17},{10,2},{18,10},{26,18},{... | collective-permute-start | bytes 786440 | tf_op jit(solution)/shard_map/ppermute | solution.py:20
  49.3 9.1 %collective-permute-start.6 = (bf16[3,1,128,256]{3,2,1,0:T(8,128)(2,1)}, bf16[3,1,128,256]{3,2,1,0:T(8,128)(2,1)}, u32[]{:S(2)}, u32[]{:S(2)}) collective-permute-start(bf16[3,1,128,256]{3,2,1,0:T(8,128)(2,1)} %get-tuple-element.265), channel_id=1, source_target_pairs={{0,1},{1,2},{2,3},{3,4},{4,5},{5,6},{6,7},{8,9},{9,10},{10,11},{11... | collective-permute-start | bytes 589832 | tf_op jit(solution)/shard_map/ppermute | solution.py:18
  54.6 5.0 %collective-permute-start.7 = (bf16[3,1,128,256]{3,2,1,0:T(8,128)(2,1)}, bf16[3,1,128,256]{3,2,1,0:T(8,128)(2,1)S(1)}, u32[]{:S(2)}, u32[]{:S(2)}) collective-permute-start(bf16[3,1,128,256]{3,2,1,0:T(8,128)(2,1)} %get-tuple-element.264), channel_id=1, source_target_pairs={{1,0},{2,1},{3,2},{4,3},{5,4},{6,5},{7,6},{9,8},{10,9},{11,10},{12... | collective-permute-start | bytes 589832 | tf_op jit(solution)/shard_map/ppermute | solution.py:20
  62.0 1.1 copy-start.9
  64.9 1.1 copy-start.6
  66.0 1.1 copy-start.22
  70.8 2.7 copy-start.12
  70.8 2.7 copy-start.16
  70.8 17.9 %copy-start.13 = (f32[2048]{0:T(1024)S(1)}, f32[2048]{0:T(1024)}, u32[]{:S(2)}) copy-start(f32[2048]{0:T(1024)} %param.24) | copy-start | bytes 24580
  90.1 1.3 copy-start.17
  90.1 1.5 copy-start.18
  90.1 1.8 copy-start.19
  90.2 1.8 copy-start.20
  98.8 87.2 %all-to-all-start = ((bf16[4,1024,256]{1,2,0:T(8,128)(2,1)}), bf16[4,1024,256]{1,2,0:T(8,128)(2,1)}, u32[]{:S(2)}, u32[]{:S(2)}) async-start(bf16[4,1024,256]{1,2,0:T(8,128)(2,1)} %tile.2), calls=%async_computation | async-start | bytes 4194304 | tf_op jit(solution)/shard_map/all_to_all | solution.py:78
  103.3 86.7 %all-gather.2.cloned.1.call-start = ((), (), s32[]{:S(2)}) async-start(), calls=%async_computation.2 | async-start | bytes 2621440 | tf_op jit(solution)/shard_map/all_gather | solution.py:75
  104.0 225.0 %reduce-scatter.2.cloned.1.call-start = ((), (), s32[]{:S(2)}) async-start(), calls=%async_computation.3 | async-start | bytes 294912 | tf_op jit(solution)/shard_map/reduce_scatter | solution.py:144
  296.0 34.4 %copy-start.1 = (bf16[128,2048]{1,0:T(8,128)(2,1)S(1)}, bf16[128,2048]{1,0:T(8,128)(2,1)}, u32[]{:S(2)}) copy-start(bf16[128,2048]{1,0:T(8,128)(2,1)} %param.23) | copy-start | bytes 1572868
  (10 other events, 9.5 us)
Sparse Core Ops, SparseCore 0:
  105.6 74.5 all-gather.1
  298.0 30.9 reduce-scatter.1
